TPU v7x, 32 devices: a whole 2x2x4 slice. The times are simulated.
32 devices in a mesh: cases: 2 (over y), runs: 16 (over z, x, core).
Axes of the slice: x: 2, y: 2, z: 4, core: 2. Of those that a mesh axis runs over, the one named last changes fastest.
Arguments:
- run_inputs: float32 [2048, 24], P(('cases', 'runs')), parts along dimension 0, may hold values from -3 to 3
- term_codes: int32 [4096, 4], replicated, may hold values from 0 to 119
- weight_levels: int32 [4096], replicated, may hold values from 0 to 3
- correlations: bfloat16 [8192, 1024], P(('cases', 'runs')), parts along dimension 0, may hold values from -32 to 32
- slab_modes: bfloat16 [4096, 1024], P('cases'), parts along dimension 0, may hold values from -0.1875 to 0.1875
- cell_map: int32 [2048], replicated, may hold values from 0 to 2047, each once
Outputs:
- coefficients: float32 [8192, 1024], P(('cases', 'runs')), parts along dimension 0
- lifted: bfloat16 [8192, 2048], P(('cases', 'runs')), parts along dimension 0
There are 2 independent parts, one for each index of `cases`. A program takes and returns all parts, laid end to end along the dimension named above; an argument that names none is the same for every part. Nothing has to cross between parts.
All inputs are finite; a program needn't handle non-finite values.
Results may differ from a plain program's by a relative error of at most 0.0067.
Values may be sent and summed in bfloat16 or wider, within the bound.
A program may use at most 64 MiB of HBM per device.

v0:
```python
import functools
import math

import jax
import jax.numpy as jnp
from jax import lax
from jax.experimental import pallas as pl
from jax.experimental.pallas import tpu as pltpu
from jax.sharding import PartitionSpec as P

STEP = 0.5
LAMBDA_FRACTION = 0.05
EPSILON = 1e-06
ROOT_TWO = math.sqrt(2.0)
ROOT_SIX = math.sqrt(6.0)
ROOT_TWENTYFOUR = math.sqrt(24.0)
DEGREES = 5
LANES = 128


def hermite_columns(points):
    squared = points * points
    return [
        jnp.ones_like(points),
        points,
        (squared - 1.0) / ROOT_TWO,
        points * (squared - 3.0) / ROOT_SIX,
        (squared * squared - 6.0 * squared + 3.0) / ROOT_TWENTYFOUR,
    ]


def hermite_table(points):
    return jnp.stack(hermite_columns(points), axis=-1).reshape(points.shape[0], -1)


def basis(points, codes):
    hermite = hermite_table(points)
    product = jnp.take(hermite, codes[:, 0], axis=1)
    for column in range(1, codes.shape[1]):
        product = product * jnp.take(hermite, codes[:, column], axis=1)
    return product.astype(jnp.bfloat16)


def shrink(values, limits):
    length = jnp.sqrt(jnp.sum(values * values, axis=1, keepdims=True) + EPSILON)
    return values * jnp.maximum(0.0, 1.0 - limits / length)


def dot_nn(left, right):
    return lax.dot_general(
        left, right, (((1,), (0,)), ((), ())), preferred_element_type=jnp.float32
    )


def dot_nt(left, right):
    return lax.dot_general(
        left, right, (((1,), (1,)), ((), ())), preferred_element_type=jnp.float32
    )


def kernel(
    n,
    corr_hbm,
    points_hbm,
    levels_hbm,
    codes_hbm,
    map_hbm,
    slab_hbm,
    coef_ref,
    lift_ref,
    points_all,
    norms_all,
    corr_ref,
    points_ref,
    levels_ref,
    codes_ref,
    map_ref,
    weights,
    blocks,
    table,
    design,
    total,
    total_in,
    fitted,
    outgoing,
    summed,
    codes,
    cells,
    slab,
    permuted,
    local_sem,
    points_send,
    points_recv,
    norms_send,
    norms_recv,
    relay_send,
    relay_recv,
    blocks_send,
    blocks_recv,
    total_send,
    total_recv,
    summed_send,
    summed_recv,
):
    me = lax.axis_index("runs")
    chips = n // 2
    chip = me // 2
    core = lax.rem(me, 2)
    terms, modes = corr_ref.shape
    width = modes // chips
    runs = table.shape[1]
    half = table.shape[0] // 2

    def peer(offset):
        return lax.rem(me + offset, n)

    def chip_at(offset):
        return lax.rem(chip + offset, chips)

    def term_rows(index):
        return pl.ds(pl.multiple_of(index * terms, terms), terms)

    def mode_lanes(index):
        return pl.ds(pl.multiple_of(index * width, width), width)

    def remote(src, dst, send, recv, target):
        return pltpu.make_async_remote_copy(
            src_ref=src,
            dst_ref=dst,
            send_sem=send,
            recv_sem=recv,
            device_id={"runs": target},
            device_id_type=pl.DeviceIdType.MESH,
        )

    barrier = pltpu.get_barrier_semaphore()
    for offset in range(1, n):
        pl.semaphore_signal(
            barrier,
            inc=1,
            device_id={"runs": peer(offset)},
            device_id_type=pl.DeviceIdType.MESH,
        )

    copies = [
        pltpu.make_async_copy(src, dst, local_sem.at[index])
        for index, (src, dst) in enumerate(
            [
                (corr_hbm, corr_ref),
                (points_hbm, points_ref),
                (levels_hbm, levels_ref),
                (codes_hbm, codes_ref),
                (map_hbm, map_ref),
                (slab_hbm, slab),
            ]
        )
    ]
    slab_copy = copies[-1]
    own_copy = pltpu.make_async_copy(
        corr_ref.at[:, mode_lanes(chip)],
        blocks.at[term_rows(chip)],
        local_sem.at[len(copies)],
    )
    for copy in copies:
        copy.start()
    for copy in copies[:2]:
        copy.wait()
    own_copy.start()

    wide = corr_ref[...].astype(jnp.float32)
    squares = wide * wide
    high = squares.astype(jnp.bfloat16)
    low = (squares - high.astype(jnp.float32)).astype(jnp.bfloat16)
    ones = jnp.ones((8, modes), jnp.bfloat16)
    norm_rows = dot_nt(ones, high) + dot_nt(ones, low)
    norms_all[core, chip] = norm_rows[0:1]
    raw = points_ref[...]
    inputs = raw.shape[0]
    points_all[core, chip] = jnp.concatenate(
        [jnp.where(core == side, raw, 0.0) for side in range(2)], axis=1
    )
    pl.semaphore_wait(barrier, n - 1)

    def points_move(offset):
        return remote(
            points_all.at[core, chip],
            points_all.at[core, chip],
            points_send.at[offset],
            points_recv.at[offset],
            chip_at(offset) * 2 + core,
        )

    def norms_move(offset):
        return remote(
            norms_all.at[core, chip],
            norms_all.at[core, chip],
            norms_send.at[offset],
            norms_recv.at[offset],
            chip_at(offset) * 2 + core,
        )

    def block_move(offset):
        there = chip_at(offset)
        return remote(
            corr_ref.at[:, mode_lanes(there)],
            blocks.at[term_rows(chip)],
            blocks_send.at[offset],
            blocks_recv.at[offset],
            there * 2 + core,
        )

    def relays():
        other = chip * 2 + (1 - core)
        mine, norms = points_all.at[core], norms_all.at[core]
        return (
            remote(mine, mine, relay_send.at[0], relay_recv.at[0], other),
            remote(norms, norms, relay_send.at[1], relay_recv.at[1], other),
        )

    def total_move():
        return remote(total, total_in, total_send, total_recv, chip * 2 + (1 - core))

    def summed_move(offset):
        there = chip_at(offset)
        return remote(
            outgoing.at[term_rows(there)],
            summed.at[:, mode_lanes(chip)],
            summed_send.at[offset],
            summed_recv.at[offset],
            there * 2 + core,
        )

    for offset in range(1, chips):
        points_move(offset).start()
    for offset in range(1, chips):
        norms_move(offset).start()
    for offset in range(1, chips):
        block_move(offset).start()

    for copy in copies[2:-1]:
        copy.wait()
    for index in range(n):
        weights[index % 2, index // 2] = jnp.exp2(
            levels_ref[index].astype(jnp.float32)
        )

    @pl.loop(0, chips)
    def _(index):
        lanes = term_rows(index * 2 + core)
        code = codes_ref[:, lanes]
        position = lax.shift_right_logical(code * 205, 10)
        code = (code - DEGREES * position) * inputs + position
        spare = jnp.zeros((8 - code.shape[0], terms), jnp.int32)
        codes[term_rows(index), :] = jnp.transpose(
            jnp.concatenate([code, spare], axis=0)
        )

    @pl.loop(0, map_ref.shape[1] // 256)
    def _(step):
        lanes = pl.ds(pl.multiple_of(step * 256, 256), 256)
        cells[lanes, :] = jnp.transpose(
            jnp.broadcast_to(map_ref[:, lanes], (8, 256))
        )

    place = lax.broadcasted_iota(jnp.int32, (256, slab.shape[0]), 1)
    chunks = cells.shape[0] // 256
    early, middle = 3 * chunks // 8, chunks // 2

    def permute(first, last):
        @pl.loop(first, last)
        def _(step):
            rows = pl.ds(pl.multiple_of(step * 256, 256), 256)
            pick = jnp.where(place == cells[rows, 0:1], 1.0, 0.0).astype(jnp.bfloat16)
            permuted[rows, :] = dot_nn(pick, slab[...]).astype(jnp.bfloat16)

    slab_copy.wait()
    permute(0, early)
    for offset in range(1, chips):
        points_move(offset).wait_recv()
        norms_move(offset).wait_recv()
    points_relay, norms_relay = relays()
    points_relay.start()
    norms_relay.start()
    permute(early, middle)
    points_relay.wait_recv()
    norms_relay.wait_recv()
    for index in range(chips):
        points = points_all[0, index] + points_all[1, index]
        columns = hermite_columns(points)
        used = DEGREES * points.shape[0]
        if used < half:
            columns.append(jnp.zeros((half - used, points.shape[1]), jnp.float32))
        values = jnp.concatenate(columns, axis=0)
        upper = values.astype(jnp.bfloat16)
        lower = (values - upper.astype(jnp.float32)).astype(jnp.bfloat16)
        lanes = slice(index * points.shape[1], (index + 1) * points.shape[1])
        table[0:half, lanes] = upper
        table[half:, lanes] = lower

    ratio = jnp.sqrt(norms_all[...]) / weights[...]
    penalty = LAMBDA_FRACTION * jnp.max(
        jnp.max(jnp.max(ratio, axis=0), axis=0), axis=1, keepdims=True
    )
    own_copy.wait()
    total[...] = jnp.zeros_like(total)
    position = lax.broadcasted_iota(jnp.int32, (terms, 2 * half), 1)
    position = jnp.where(position >= half, position - half, position)
    piece = min(256, runs)

    @pl.loop(0, chips)
    def _(offset):
        there = lax.rem(chip - offset + chips, chips)
        rows = term_rows(there)
        picks = [
            jnp.where(position == codes[rows, slot : slot + 1], 1.0, 0.0).astype(
                jnp.bfloat16
            )
            for slot in range(codes_ref.shape[0])
        ]
        for start in range(0, runs, piece):
            lanes = slice(start, start + piece)
            product = dot_nn(picks[0], table[:, lanes])
            for pick in picks[1:]:
                product = product * dot_nn(pick, table[:, lanes])
            design[rows, lanes] = product.astype(jnp.bfloat16)

        @pl.when(offset > 0)
        def _():
            block_move(offset).wait_recv()

        length = jnp.sqrt(STEP * STEP * norms_all[core, there] + EPSILON)
        limits = STEP * penalty * weights[core, there]
        factor = jnp.maximum(0.0, 1.0 - limits / length)
        turned = jnp.transpose(blocks[rows, :].astype(jnp.float32))
        first_half = (STEP * turned * factor).astype(jnp.bfloat16)
        total[...] += dot_nn(first_half, design[rows, :])

    total_move().start()
    total_move().wait_recv()
    fitted[...] = (total[...] + total_in[...]).astype(jnp.bfloat16)

    @pl.loop(1, chips)
    def _(offset):
        rows = term_rows(chip_at(offset))
        outgoing[rows, :] = dot_nt(design[rows, :], fitted[...]).astype(jnp.bfloat16)
        summed_move(offset).start()

    summed[:, mode_lanes(chip)] = dot_nt(
        design[term_rows(chip), :], fitted[...]
    ).astype(jnp.bfloat16)

    permute(middle, chunks)
    own_limits = jnp.broadcast_to(STEP * penalty * weights[core, chip], (8, terms))
    limits = jnp.transpose(own_limits)[:, 0:1]
    corr = corr_ref[...].astype(jnp.float32)
    first = shrink(STEP * corr, limits)
    for offset in range(1, chips):
        summed_move(offset).wait_recv()
    gradient = summed[...].astype(jnp.float32) / runs - corr
    coefficients = shrink(first - STEP * gradient, limits)
    coef_ref[...] = coefficients
    narrow = coefficients.astype(jnp.bfloat16)
    for start in range(0, cells.shape[0], 512):
        lanes = slice(start, start + 512)
        lift_ref[:, lanes] = dot_nt(narrow, permuted[lanes, :]).astype(jnp.bfloat16)

    points_relay.wait_send()
    norms_relay.wait_send()
    for offset in range(1, chips):
        points_move(offset).wait_send()
        norms_move(offset).wait_send()
        block_move(offset).wait_send()
        summed_move(offset).wait_send()
    total_move().wait_send()


def finish(coef_in, lift_in, coef_ref, lift_ref):
    coef_ref[...] = coef_in[...]
    lift_ref[...] = lift_in[...]


def by_chips(run_inputs, term_codes, weight_levels, correlations, slab_modes, cell_map):
    run_count, inputs = run_inputs.shape
    terms, modes = correlations.shape
    n = lax.axis_size("runs")
    chips = n // 2
    runs = run_count * n
    count = cell_map.shape[0]
    width = modes // chips
    lane_terms = chips * terms
    half = -(-DEGREES * inputs // LANES) * LANES
    f32, bf16 = jnp.float32, jnp.bfloat16
    vmem = pl.BlockSpec(memory_space=pltpu.VMEM)
    hbm = pl.BlockSpec(memory_space=pltpu.HBM)
    dma = pltpu.SemaphoreType.DMA
    coefficients, lifted = pl.pallas_call(
        functools.partial(kernel, n),
        out_shape=(
            jax.ShapeDtypeStruct((terms, modes), f32),
            jax.ShapeDtypeStruct((terms, count), bf16),
        ),
        in_specs=[hbm] * 6,
        out_specs=(vmem, vmem),
        scratch_shapes=[
            pltpu.VMEM((2, chips, inputs, 2 * run_count), f32),
            pltpu.VMEM((2, chips, 1, terms), f32),
            pltpu.VMEM((terms, modes), bf16),
            pltpu.VMEM((inputs, run_count), f32),
            pltpu.VMEM((n, 1, terms), jnp.int32),
            pltpu.VMEM((term_codes.shape[1], n * terms), jnp.int32),
            pltpu.VMEM((1, count), jnp.int32),
            pltpu.VMEM((2, chips, 1, terms), f32),
            pltpu.VMEM((lane_terms, width), bf16),
            pltpu.VMEM((2 * half, runs), bf16),
            pltpu.VMEM((lane_terms, runs), bf16),
            pltpu.VMEM((width, runs), f32),
            pltpu.VMEM((width, runs), f32),
            pltpu.VMEM((width, runs), bf16),
            pltpu.VMEM((lane_terms, width), bf16),
            pltpu.VMEM((terms, modes), bf16),
            pltpu.VMEM((lane_terms, 8), jnp.int32),
            pltpu.VMEM((count, 8), jnp.int32),
            pltpu.VMEM(slab_modes.shape, bf16),
            pltpu.VMEM((count, modes), bf16),
            dma((7,)),
            dma((chips,)),
            dma((chips,)),
            dma((chips,)),
            dma((chips,)),
            dma((2,)),
            dma((7,)),
            dma((chips,)),
            dma((chips,)),
            dma,
            dma,
            dma((chips,)),
            dma((chips,)),
        ],
        compiler_params=pltpu.CompilerParams(
            collective_id=0, has_side_effects=True, vmem_limit_bytes=40 * 2**20
        ),
    )(
        *[
            pltpu.with_memory_space_constraint(array, pltpu.HBM)
            for array in (
                correlations,
                run_inputs.T,
                weight_levels.reshape(n, 1, terms),
                term_codes.T,
                cell_map.reshape(1, count),
                slab_modes,
            )
        ]
    )
    rows = terms // 4
    specs = (
        pl.BlockSpec((rows, modes), lambda step: (step, 0)),
        pl.BlockSpec((rows, count), lambda step: (step, 0)),
    )
    return pl.pallas_call(
        finish,
        grid=(4,),
        out_shape=(
            jax.ShapeDtypeStruct((terms, modes), f32),
            jax.ShapeDtypeStruct((terms, count), bf16),
        ),
        in_specs=list(specs),
        out_specs=specs,
        compiler_params=pltpu.CompilerParams(vmem_limit_bytes=8 * 2**20),
    )(coefficients, lifted)


def by_gathers(
    run_inputs, term_codes, weight_levels, correlations, slab_modes, cell_map
):
    run_count = run_inputs.shape[0]
    term_count = correlations.shape[0]
    devices = lax.axis_size("runs")
    offset = lax.axis_index("runs") * term_count
    total_runs = run_count * devices
    weights_all = jnp.exp2(weight_levels.astype(jnp.float32))
    own_weights = lax.dynamic_slice_in_dim(weights_all, offset, term_count)
    own_corr = correlations.astype(jnp.float32)
    ratio = jnp.max(jnp.sqrt(jnp.sum(own_corr * own_corr, axis=1)) / own_weights)
    penalty = LAMBDA_FRACTION * lax.pmax(ratio, "runs")
    limits = (STEP * penalty * own_weights)[:, None]
    first = shrink(STEP * own_corr, limits)
    design = basis(run_inputs, term_codes)
    fitted = dot_nn(
        design,
        lax.all_gather(first.astype(jnp.bfloat16), "runs", axis=0, tiled=True),
    )
    fitted_half = fitted.astype(jnp.bfloat16)
    all_points = lax.all_gather(run_inputs, "runs", axis=0, tiled=True)
    own_codes = lax.dynamic_slice_in_dim(term_codes, offset, term_count, 0)
    owned_design = basis(all_points, own_codes)
    summed = lax.dot_general(
        owned_design,
        lax.all_gather(fitted_half, "runs", axis=0, tiled=True),
        (((0,), (0,)), ((), ())),
        preferred_element_type=jnp.float32,
    )
    gradient = summed / total_runs - own_corr
    coefficients = shrink(first - STEP * gradient, limits)
    modes = jnp.take(slab_modes, cell_map, axis=0)
    lifted = dot_nt(coefficients.astype(jnp.bfloat16), modes).astype(jnp.bfloat16)
    return (coefficients, lifted)


def on_device(run_inputs, term_codes, weight_levels, correlations, slab_modes, cell_map):
    n = lax.axis_size("runs")
    terms, modes = correlations.shape
    aligned = (
        n % 2 == 0
        and modes % (LANES * max(n // 2, 1)) == 0
        and terms % LANES == 0
        and term_codes.shape[1] <= 8
        and DEGREES * run_inputs.shape[1] < 1024
        and (2 * run_inputs.shape[0]) % LANES == 0
        and run_inputs.shape[1] % 8 == 0
        and cell_map.shape[0] % 512 == 0
        and (run_inputs.shape[0] * n) % 256 == 0
    )
    step = by_chips if aligned else by_gathers
    return step(
        run_inputs, term_codes, weight_levels, correlations, slab_modes, cell_map
    )


def solution(mesh):
    return jax.shard_map(
        on_device,
        mesh=mesh,
        in_specs=(
            P(("cases", "runs"), None),
            P(),
            P(),
            P(("cases", "runs"), None),
            P("cases", None),
            P(),
        ),
        out_specs=(P(("cases", "runs"), None), P(("cases", "runs"), None)),
        check_vma=False,
    )
```

profile of v0, /device:TPU:27, one launch (start us, length us, event | category | flops | bytes accessed | tf_op | source)
XLA Modules:
  0.0 43.6 jit_solution(15158608882006662130)
XLA Ops:
  0.6 41.1 %shard_map.77 = (f32[256,1024]{1,0:T(8,128)S(1)}, bf16[256,2048]{1,0:T(8,128)(2,1)S(1)}) custom-call(bf16[256,1024]{1,0:T(8,128)(2,1)} %corr_hbm.1, f32[24,64]{1,0:T(8,128)} %bitcast.6, s32[16,1,256]{2,1,0:T(1,128)} %bitcast.5, s32[4,4096]{1,0:T(4,128)} %bitcast.4, s32[1,2048]{1,0:T(1,128)} %bitcast.7, bf16[2048,1024]{1,0:T(8,128)(2,1)} %slab_hbm.1), custom_call_target="tpu_custom_call" | custom-call | tf_op jit(solution)/shard_map/pallas_call | solution.py:396
  41.8 1.8 %shard_map.78 = (f32[256,1024]{1,0:T(8,128)}, bf16[256,2048]{1,0:T(8,128)(2,1)}) custom-call(f32[256,1024]{1,0:T(8,128)S(1)} %get-tuple-element.4.coef_in, bf16[256,2048]{1,0:T(8,128)(2,1)S(1)} %get-tuple-element.5.lift_in), custom_call_target="tpu_custom_call" | custom-call | tf_op jit(solution)/shard_map/pallas_call | solution.py:460
where the time goes:
time: 43.8 us; the launch traced here: 43.6 us
  Pallas kernels  43 us (98%)
  between operations  0.64 us (1%)
    pallas_call x1, Pallas kernels, by_chips(): pl.pallas_call(functools.partial(kernel, n), out_shape=(jax.ShapeDtypeStr...  41.1 us
    pallas_call x1, Pallas kernels, by_chips(): pl.pallas_call(finish, grid=(4,), out_shape=(jax.ShapeDtypeStruct((terms,...  1.85 us

commit v1 on v0

--- a/solution.py
+++ b/solution.py
@@ -67,7 +67,7 @@
     map_hbm,
     slab_hbm,
     coef_ref,
-    lift_ref,
+    permuted,
     points_all,
     norms_all,
     corr_ref,
@@ -87,7 +87,6 @@
     codes,
     cells,
     slab,
-    permuted,
     local_sem,
     points_send,
     points_recv,
@@ -110,12 +109,27 @@
     width = modes // chips
     runs = table.shape[1]
     half = table.shape[0] // 2
+    side = chips // 2
+    low_side = chip < side
+    inner = jnp.logical_and(chip >= side // 2, chip < chips - side // 2)
 
     def peer(offset):
         return lax.rem(me + offset, n)
 
     def chip_at(offset):
         return lax.rem(chip + offset, chips)
+
+    def near_chip(step):
+        base = chip // side * side
+        return base + lax.rem(chip - base + step, side)
+
+    def far_chip(step):
+        row = step // 2
+        row = jnp.where(low_side, side - 1 - row, row)
+        return 2 * row + lax.rem(chip + 1 + step, 2)
+
+    def offset_to(there):
+        return lax.rem(there - chip + chips, chips)
 
     def term_rows(index):
         return pl.ds(pl.multiple_of(index * terms, terms), terms)
@@ -230,12 +244,19 @@
             there * 2 + core,
         )
 
-    for offset in range(1, chips):
-        points_move(offset).start()
-    for offset in range(1, chips):
-        norms_move(offset).start()
-    for offset in range(1, chips):
-        block_move(offset).start()
+    targets = [far_chip(step) for step in range(side)]
+    targets += [near_chip(step) for step in range(1, side)]
+    for there in targets:
+        points_move(offset_to(there)).start()
+    for there in targets:
+        norms_move(offset_to(there)).start()
+    def send_far():
+        for step in range(side):
+            block_move(offset_to(far_chip(step))).start()
+
+    pl.when(inner)(send_far)
+    for step in range(1, side):
+        block_move(offset_to(near_chip(step))).start()
 
     for copy in copies[2:-1]:
         copy.wait()
@@ -244,27 +265,27 @@
             levels_ref[index].astype(jnp.float32)
         )
 
-    @pl.loop(0, chips)
-    def _(index):
+    for index in range(chips):
         lanes = term_rows(index * 2 + core)
         code = codes_ref[:, lanes]
         position = lax.shift_right_logical(code * 205, 10)
         code = (code - DEGREES * position) * inputs + position
         spare = jnp.zeros((8 - code.shape[0], terms), jnp.int32)
-        codes[term_rows(index), :] = jnp.transpose(
+        codes[index * terms : (index + 1) * terms, :] = jnp.transpose(
             jnp.concatenate([code, spare], axis=0)
         )
 
-    @pl.loop(0, map_ref.shape[1] // 256)
-    def _(step):
-        lanes = pl.ds(pl.multiple_of(step * 256, 256), 256)
+    for start in range(0, map_ref.shape[1], 256):
+        lanes = slice(start, start + 256)
         cells[lanes, :] = jnp.transpose(
             jnp.broadcast_to(map_ref[:, lanes], (8, 256))
         )
 
+    pl.when(jnp.logical_not(inner))(send_far)
+
     place = lax.broadcasted_iota(jnp.int32, (256, slab.shape[0]), 1)
     chunks = cells.shape[0] // 256
-    early, middle = 3 * chunks // 8, chunks // 2
+    early, middle = chunks // 4, 3 * chunks // 8
 
     def permute(first, last):
         @pl.loop(first, last)
@@ -307,9 +328,11 @@
     position = jnp.where(position >= half, position - half, position)
     piece = min(256, runs)
 
-    @pl.loop(0, chips)
-    def _(offset):
-        there = lax.rem(chip - offset + chips, chips)
+    @pl.loop(0, chips, unroll=2)
+    def _(step):
+        there = jnp.where(
+            step < side, near_chip(step), far_chip(chips - 1 - lax.max(step, side))
+        )
         rows = term_rows(there)
         picks = [
             jnp.where(position == codes[rows, slot : slot + 1], 1.0, 0.0).astype(
@@ -324,9 +347,9 @@
                 product = product * dot_nn(pick, table[:, lanes])
             design[rows, lanes] = product.astype(jnp.bfloat16)
 
-        @pl.when(offset > 0)
+        @pl.when(step > 0)
         def _():
-            block_move(offset).wait_recv()
+            block_move(lax.rem(chip - there + chips, chips)).wait_recv()
 
         length = jnp.sqrt(STEP * STEP * norms_all[core, there] + EPSILON)
         limits = STEP * penalty * weights[core, there]
@@ -340,10 +363,13 @@
     fitted[...] = (total[...] + total_in[...]).astype(jnp.bfloat16)
 
     @pl.loop(1, chips)
-    def _(offset):
-        rows = term_rows(chip_at(offset))
+    def _(step):
+        there = jnp.where(
+            step <= side, far_chip(lax.min(step, side) - 1), near_chip(step - side)
+        )
+        rows = term_rows(there)
         outgoing[rows, :] = dot_nt(design[rows, :], fitted[...]).astype(jnp.bfloat16)
-        summed_move(offset).start()
+        summed_move(offset_to(there)).start()
 
     summed[:, mode_lanes(chip)] = dot_nt(
         design[term_rows(chip), :], fitted[...]
@@ -359,10 +385,6 @@
     gradient = summed[...].astype(jnp.float32) / runs - corr
     coefficients = shrink(first - STEP * gradient, limits)
     coef_ref[...] = coefficients
-    narrow = coefficients.astype(jnp.bfloat16)
-    for start in range(0, cells.shape[0], 512):
-        lanes = slice(start, start + 512)
-        lift_ref[:, lanes] = dot_nt(narrow, permuted[lanes, :]).astype(jnp.bfloat16)
 
     points_relay.wait_send()
     norms_relay.wait_send()
@@ -374,9 +396,14 @@
     total_move().wait_send()
 
 
-def finish(coef_in, lift_in, coef_ref, lift_ref):
-    coef_ref[...] = coef_in[...]
-    lift_ref[...] = lift_in[...]
+def finish(coef_in, permuted, coef_ref, lift_ref):
+    step = pl.program_id(0)
+    rows, width = coef_ref.shape[0], lift_ref.shape[1]
+    own = pl.ds(pl.multiple_of(step * rows, rows), rows)
+    coef_ref[...] = coef_in[own, :]
+    cells = pl.ds(pl.multiple_of(step * width, width), width)
+    narrow = coef_in[...].astype(jnp.bfloat16)
+    lift_ref[...] = dot_nt(narrow, permuted[cells, :]).astype(jnp.bfloat16)
 
 
 def by_chips(run_inputs, term_codes, weight_levels, correlations, slab_modes, cell_map):
@@ -393,11 +420,11 @@
     vmem = pl.BlockSpec(memory_space=pltpu.VMEM)
     hbm = pl.BlockSpec(memory_space=pltpu.HBM)
     dma = pltpu.SemaphoreType.DMA
-    coefficients, lifted = pl.pallas_call(
+    coefficients, permuted = pl.pallas_call(
         functools.partial(kernel, n),
         out_shape=(
             jax.ShapeDtypeStruct((terms, modes), f32),
-            jax.ShapeDtypeStruct((terms, count), bf16),
+            jax.ShapeDtypeStruct((count, modes), bf16),
         ),
         in_specs=[hbm] * 6,
         out_specs=(vmem, vmem),
@@ -421,7 +448,6 @@
             pltpu.VMEM((lane_terms, 8), jnp.int32),
             pltpu.VMEM((count, 8), jnp.int32),
             pltpu.VMEM(slab_modes.shape, bf16),
-            pltpu.VMEM((count, modes), bf16),
             dma((7,)),
             dma((chips,)),
             dma((chips,)),
@@ -452,22 +478,21 @@
             )
         ]
     )
-    rows = terms // 4
-    specs = (
-        pl.BlockSpec((rows, modes), lambda step: (step, 0)),
-        pl.BlockSpec((rows, count), lambda step: (step, 0)),
-    )
+    steps = 4
     return pl.pallas_call(
         finish,
-        grid=(4,),
+        grid=(steps,),
         out_shape=(
             jax.ShapeDtypeStruct((terms, modes), f32),
             jax.ShapeDtypeStruct((terms, count), bf16),
         ),
-        in_specs=list(specs),
-        out_specs=specs,
+        in_specs=[vmem, vmem],
+        out_specs=(
+            pl.BlockSpec((terms // steps, modes), lambda step: (step, 0)),
+            pl.BlockSpec((terms, count // steps), lambda step: (0, step)),
+        ),
         compiler_params=pltpu.CompilerParams(vmem_limit_bytes=8 * 2**20),
-    )(coefficients, lifted)
+    )(coefficients, permuted)
 
 
 def by_gathers(
@@ -511,7 +536,7 @@
     n = lax.axis_size("runs")
     terms, modes = correlations.shape
     aligned = (
-        n % 2 == 0
+        n % 8 == 0
         and modes % (LANES * max(n // 2, 1)) == 0
         and terms % LANES == 0
         and term_codes.shape[1] <= 8

time: 43.8 us -> 41.4 us (0.945)
  the two profiles are of different devices: /device:TPU:27 before, /device:TPU:9 now
where the time goes in v1:
time: 41.4 us; the launch traced here: 41 us
  Pallas kernels  40.3 us (97%)
  between operations  0.64 us (2%)
    pallas_call x1, Pallas kernels, by_chips(): pl.pallas_call(functools.partial(kernel, n), out_shape=(jax.ShapeDtypeStr...  37.4 us
    pallas_call x1, Pallas kernels, by_chips(): pl.pallas_call(finish, grid=(steps,), out_shape=(jax.ShapeDtypeStruct((te...  2.92 us

profile of v1, /device:TPU:9, one launch (start us, length us, event | category | flops | bytes accessed | tf_op | source)
XLA Modules:
  0.0 41.0 jit_solution(8428801655618187729)
XLA Ops:
  0.6 37.4 %shard_map.77 = (f32[256,1024]{1,0:T(8,128)S(1)}, bf16[2048,1024]{1,0:T(8,128)(2,1)S(1)}) custom-call(bf16[256,1024]{1,0:T(8,128)(2,1)} %corr_hbm.1, f32[24,64]{1,0:T(8,128)} %bitcast.6, s32[16,1,256]{2,1,0:T(1,128)} %bitcast.5, s32[4,4096]{1,0:T(4,128)} %bitcast.4, s32[1,2048]{1,0:T(1,128)} %bitcast.7, bf16[2048,1024]{1,0:T(8,128)(2,1)} %slab_hbm.1), custom_call_target="tpu_custom_call" | custom-call | tf_op jit(solution)/shard_map/pallas_call | solution.py:423
  38.1 2.9 %shard_map.78 = (f32[256,1024]{1,0:T(8,128)}, bf16[256,2048]{1,0:T(8,128)(2,1)}) custom-call(f32[256,1024]{1,0:T(8,128)S(1)} %get-tuple-element.4.coef_in, bf16[2048,1024]{1,0:T(8,128)(2,1)S(1)} %get-tuple-element.5.permuted), custom_call_target="tpu_custom_call" | custom-call | tf_op jit(solution)/shard_map/pallas_call | solution.py:482

commit v2 on v1

--- a/solution.py
+++ b/solution.py
@@ -68,8 +68,9 @@
     slab_hbm,
     coef_ref,
     permuted,
+    packets,
+    norms_all,
     points_all,
-    norms_all,
     corr_ref,
     points_ref,
     levels_ref,
@@ -88,10 +89,8 @@
     cells,
     slab,
     local_sem,
-    points_send,
-    points_recv,
-    norms_send,
-    norms_recv,
+    packets_send,
+    packets_recv,
     relay_send,
     relay_recv,
     blocks_send,
@@ -187,29 +186,25 @@
     low = (squares - high.astype(jnp.float32)).astype(jnp.bfloat16)
     ones = jnp.ones((8, modes), jnp.bfloat16)
     norm_rows = dot_nt(ones, high) + dot_nt(ones, low)
-    norms_all[core, chip] = norm_rows[0:1]
-    raw = points_ref[...]
-    inputs = raw.shape[0]
-    points_all[core, chip] = jnp.concatenate(
-        [jnp.where(core == side, raw, 0.0) for side in range(2)], axis=1
-    )
+    inputs = points_ref.shape[0]
+    fold = inputs // 2
+    norm_lanes = [
+        (fold + start // LANES, slice(start, start + LANES))
+        for start in range(0, terms, LANES)
+    ]
+    packets[core, chip, 0:fold] = jnp.concatenate(
+        [points_ref[0:fold], points_ref[fold:inputs]], axis=1
+    )
+    for row, lanes in norm_lanes:
+        packets[core, chip, row : row + 1] = norm_rows[0:1, lanes]
     pl.semaphore_wait(barrier, n - 1)
 
-    def points_move(offset):
+    def packet_move(offset):
         return remote(
-            points_all.at[core, chip],
-            points_all.at[core, chip],
-            points_send.at[offset],
-            points_recv.at[offset],
-            chip_at(offset) * 2 + core,
-        )
-
-    def norms_move(offset):
-        return remote(
-            norms_all.at[core, chip],
-            norms_all.at[core, chip],
-            norms_send.at[offset],
-            norms_recv.at[offset],
+            packets.at[core, chip],
+            packets.at[core, chip],
+            packets_send.at[offset],
+            packets_recv.at[offset],
             chip_at(offset) * 2 + core,
         )
 
@@ -223,13 +218,9 @@
             there * 2 + core,
         )
 
-    def relays():
-        other = chip * 2 + (1 - core)
-        mine, norms = points_all.at[core], norms_all.at[core]
-        return (
-            remote(mine, mine, relay_send.at[0], relay_recv.at[0], other),
-            remote(norms, norms, relay_send.at[1], relay_recv.at[1], other),
-        )
+    def relay():
+        mine = packets.at[core]
+        return remote(mine, mine, relay_send, relay_recv, chip * 2 + (1 - core))
 
     def total_move():
         return remote(total, total_in, total_send, total_recv, chip * 2 + (1 - core))
@@ -247,9 +238,7 @@
     targets = [far_chip(step) for step in range(side)]
     targets += [near_chip(step) for step in range(1, side)]
     for there in targets:
-        points_move(offset_to(there)).start()
-    for there in targets:
-        norms_move(offset_to(there)).start()
+        packet_move(offset_to(there)).start()
     def send_far():
         for step in range(side):
             block_move(offset_to(far_chip(step))).start()
@@ -297,16 +286,23 @@
     slab_copy.wait()
     permute(0, early)
     for offset in range(1, chips):
-        points_move(offset).wait_recv()
-        norms_move(offset).wait_recv()
-    points_relay, norms_relay = relays()
-    points_relay.start()
-    norms_relay.start()
+        packet_move(offset).wait_recv()
+    packets_relay = relay()
+    packets_relay.start()
     permute(early, middle)
-    points_relay.wait_recv()
-    norms_relay.wait_recv()
+    packets_relay.wait_recv()
+    first_core = lax.broadcasted_iota(jnp.int32, (fold, LANES), 1) < LANES // 2
     for index in range(chips):
-        points = points_all[0, index] + points_all[1, index]
+        even, odd = (packets[side, index, 0:fold] for side in range(2))
+        turned = pltpu.roll(odd, LANES // 2, 1)
+        points_all[index, 0:fold] = jnp.where(first_core, even, turned)
+        turned = pltpu.roll(even, LANES // 2, 1)
+        points_all[index, fold:inputs] = jnp.where(first_core, turned, odd)
+        for which in range(2):
+            for row, lanes in norm_lanes:
+                norms_all[which, index, :, lanes] = packets[which, index, row : row + 1]
+    for index in range(chips):
+        points = points_all[index]
         columns = hermite_columns(points)
         used = DEGREES * points.shape[0]
         if used < half:
@@ -328,11 +324,7 @@
     position = jnp.where(position >= half, position - half, position)
     piece = min(256, runs)
 
-    @pl.loop(0, chips, unroll=2)
-    def _(step):
-        there = jnp.where(
-            step < side, near_chip(step), far_chip(chips - 1 - lax.max(step, side))
-        )
+    def build(there):
         rows = term_rows(there)
         picks = [
             jnp.where(position == codes[rows, slot : slot + 1], 1.0, 0.0).astype(
@@ -347,10 +339,8 @@
                 product = product * dot_nn(pick, table[:, lanes])
             design[rows, lanes] = product.astype(jnp.bfloat16)
 
-        @pl.when(step > 0)
-        def _():
-            block_move(lax.rem(chip - there + chips, chips)).wait_recv()
-
+    def fit(there):
+        rows = term_rows(there)
         length = jnp.sqrt(STEP * STEP * norms_all[core, there] + EPSILON)
         limits = STEP * penalty * weights[core, there]
         factor = jnp.maximum(0.0, 1.0 - limits / length)
@@ -358,6 +348,24 @@
         first_half = (STEP * turned * factor).astype(jnp.bfloat16)
         total[...] += dot_nn(first_half, design[rows, :])
 
+    def wait_block(there):
+        block_move(lax.rem(chip - there + chips, chips)).wait_recv()
+
+    @pl.loop(0, side, unroll=2)
+    def _(step):
+        there = near_chip(step)
+        build(there)
+        pl.when(step > 0)(lambda: wait_block(there))
+        fit(there)
+
+    @pl.loop(0, side, unroll=2)
+    def _(step):
+        build(far_chip(step))
+
+    for step in range(side):
+        wait_block(far_chip(side - 1 - step))
+        fit(far_chip(side - 1 - step))
+
     total_move().start()
     total_move().wait_recv()
     fitted[...] = (total[...] + total_in[...]).astype(jnp.bfloat16)
@@ -378,19 +386,21 @@
     permute(middle, chunks)
     own_limits = jnp.broadcast_to(STEP * penalty * weights[core, chip], (8, terms))
     limits = jnp.transpose(own_limits)[:, 0:1]
-    corr = corr_ref[...].astype(jnp.float32)
-    first = shrink(STEP * corr, limits)
+    chunk = 32
+    for start in range(0, terms, chunk):
+        rows = slice(start, start + chunk)
+        half_corr = STEP * corr_ref[rows].astype(jnp.float32)
+        coef_ref[rows] = shrink(half_corr, limits[rows]) + half_corr
     for offset in range(1, chips):
         summed_move(offset).wait_recv()
-    gradient = summed[...].astype(jnp.float32) / runs - corr
-    coefficients = shrink(first - STEP * gradient, limits)
-    coef_ref[...] = coefficients
-
-    points_relay.wait_send()
-    norms_relay.wait_send()
+    for start in range(0, terms, chunk):
+        rows = slice(start, start + chunk)
+        step_sum = summed[rows].astype(jnp.float32) * (STEP / runs)
+        coef_ref[rows] = shrink(coef_ref[rows] - step_sum, limits[rows])
+
+    packets_relay.wait_send()
     for offset in range(1, chips):
-        points_move(offset).wait_send()
-        norms_move(offset).wait_send()
+        packet_move(offset).wait_send()
         block_move(offset).wait_send()
         summed_move(offset).wait_send()
     total_move().wait_send()
@@ -415,6 +425,7 @@
     count = cell_map.shape[0]
     width = modes // chips
     lane_terms = chips * terms
+    packet = -(-(inputs // 2 + terms // LANES) // 8) * 8
     half = -(-DEGREES * inputs // LANES) * LANES
     f32, bf16 = jnp.float32, jnp.bfloat16
     vmem = pl.BlockSpec(memory_space=pltpu.VMEM)
@@ -429,8 +440,9 @@
         in_specs=[hbm] * 6,
         out_specs=(vmem, vmem),
         scratch_shapes=[
-            pltpu.VMEM((2, chips, inputs, 2 * run_count), f32),
+            pltpu.VMEM((2, chips, packet, LANES), f32),
             pltpu.VMEM((2, chips, 1, terms), f32),
+            pltpu.VMEM((chips, inputs, LANES), f32),
             pltpu.VMEM((terms, modes), bf16),
             pltpu.VMEM((inputs, run_count), f32),
             pltpu.VMEM((n, 1, terms), jnp.int32),
@@ -451,10 +463,8 @@
             dma((7,)),
             dma((chips,)),
             dma((chips,)),
-            dma((chips,)),
-            dma((chips,)),
-            dma((2,)),
-            dma((7,)),
+            dma,
+            dma,
             dma((chips,)),
             dma((chips,)),
             dma,
@@ -541,7 +551,7 @@
         and terms % LANES == 0
         and term_codes.shape[1] <= 8
         and DEGREES * run_inputs.shape[1] < 1024
-        and (2 * run_inputs.shape[0]) % LANES == 0
+        and 2 * run_inputs.shape[0] == LANES
         and run_inputs.shape[1] % 8 == 0
         and cell_map.shape[0] % 512 == 0
         and (run_inputs.shape[0] * n) % 256 == 0

time: 41.4 us -> 38.5 us (0.930)
  Pallas kernels: 40.3 us -> 37.7 us
    pallas_call x1, Pallas kernels: 37.4 us -> 34.8 us  [by_chips(): pl.pallas_call(functools.partial(kernel, n), out_shape=(jax.ShapeDtypeStr...]
where the time goes in v2:
time: 38.5 us; the launch traced here: 38.4 us
  Pallas kernels  37.7 us (98%)
  between operations  0.64 us (2%)
    pallas_call x1, Pallas kernels, by_chips(): pl.pallas_call(functools.partial(kernel, n), out_shape=(jax.ShapeDtypeStr...  34.8 us
    pallas_call x1, Pallas kernels, by_chips(): pl.pallas_call(finish, grid=(steps,), out_shape=(jax.ShapeDtypeStruct((te...  2.91 us

profile of v2, /device:TPU:9, one launch (start us, length us, event | category | flops | bytes accessed | tf_op | source)
XLA Modules:
  0.0 38.4 jit_solution(6338806194931288037)
XLA Ops:
  0.6 34.8 %shard_map.77 = (f32[256,1024]{1,0:T(8,128)S(1)}, bf16[2048,1024]{1,0:T(8,128)(2,1)S(1)}) custom-call(bf16[256,1024]{1,0:T(8,128)(2,1)} %corr_hbm.1, f32[24,64]{1,0:T(8,128)} %bitcast.6, s32[16,1,256]{2,1,0:T(1,128)} %bitcast.5, s32[4,4096]{1,0:T(4,128)} %bitcast.4, s32[1,2048]{1,0:T(1,128)} %bitcast.7, bf16[2048,1024]{1,0:T(8,128)(2,1)} %slab_hbm.1), custom_call_target="tpu_custom_call" | custom-call | tf_op jit(solution)/shard_map/pallas_call | solution.py:434
  35.5 2.9 %shard_map.78 = (f32[256,1024]{1,0:T(8,128)}, bf16[256,2048]{1,0:T(8,128)(2,1)}) custom-call(f32[256,1024]{1,0:T(8,128)S(1)} %get-tuple-element.4.coef_in, bf16[2048,1024]{1,0:T(8,128)(2,1)S(1)} %get-tuple-element.5.permuted), custom_call_target="tpu_custom_call" | custom-call | tf_op jit(solution)/shard_map/pallas_call | solution.py:492

commit v3 on v2

--- a/solution.py
+++ b/solution.py
@@ -67,6 +67,7 @@
     map_hbm,
     slab_hbm,
     coef_ref,
+    narrow_ref,
     permuted,
     packets,
     norms_all,
@@ -274,7 +275,7 @@
 
     place = lax.broadcasted_iota(jnp.int32, (256, slab.shape[0]), 1)
     chunks = cells.shape[0] // 256
-    early, middle = chunks // 4, 3 * chunks // 8
+    early, middle = chunks // 8, chunks // 4
 
     def permute(first, last):
         @pl.loop(first, last)
@@ -351,17 +352,14 @@
     def wait_block(there):
         block_move(lax.rem(chip - there + chips, chips)).wait_recv()
 
-    @pl.loop(0, side, unroll=2)
+    @pl.loop(0, chips, unroll=2)
     def _(step):
-        there = near_chip(step)
-        build(there)
-        pl.when(step > 0)(lambda: wait_block(there))
-        fit(there)
-
-    @pl.loop(0, side, unroll=2)
-    def _(step):
-        build(far_chip(step))
-
+        build(step)
+
+    fit(chip)
+    for step in range(1, side):
+        wait_block(near_chip(step))
+        fit(near_chip(step))
     for step in range(side):
         wait_block(far_chip(side - 1 - step))
         fit(far_chip(side - 1 - step))
@@ -396,7 +394,9 @@
     for start in range(0, terms, chunk):
         rows = slice(start, start + chunk)
         step_sum = summed[rows].astype(jnp.float32) * (STEP / runs)
-        coef_ref[rows] = shrink(coef_ref[rows] - step_sum, limits[rows])
+        coefficients = shrink(coef_ref[rows] - step_sum, limits[rows])
+        coef_ref[rows] = coefficients
+        narrow_ref[rows] = coefficients.astype(jnp.bfloat16)
 
     packets_relay.wait_send()
     for offset in range(1, chips):
@@ -406,14 +406,20 @@
     total_move().wait_send()
 
 
-def finish(coef_in, permuted, coef_ref, lift_ref):
-    step = pl.program_id(0)
-    rows, width = coef_ref.shape[0], lift_ref.shape[1]
-    own = pl.ds(pl.multiple_of(step * rows, rows), rows)
-    coef_ref[...] = coef_in[own, :]
-    cells = pl.ds(pl.multiple_of(step * width, width), width)
-    narrow = coef_in[...].astype(jnp.bfloat16)
-    lift_ref[...] = dot_nt(narrow, permuted[cells, :]).astype(jnp.bfloat16)
+def finish(coef_in, narrow, permuted, coef_hbm, lift_hbm, lift, sems):
+    copies = [pltpu.make_async_copy(coef_in, coef_hbm, sems.at[0])]
+    copies[0].start()
+    parts, _, width = lift.shape
+    for part in range(parts):
+        lanes = slice(part * width, (part + 1) * width)
+        lift[part] = dot_nt(narrow[...], permuted[lanes]).astype(jnp.bfloat16)
+        copy = pltpu.make_async_copy(
+            lift.at[part], lift_hbm.at[:, lanes], sems.at[part + 1]
+        )
+        copy.start()
+        copies.append(copy)
+    for copy in copies:
+        copy.wait()
 
 
 def by_chips(run_inputs, term_codes, weight_levels, correlations, slab_modes, cell_map):
@@ -431,14 +437,15 @@
     vmem = pl.BlockSpec(memory_space=pltpu.VMEM)
     hbm = pl.BlockSpec(memory_space=pltpu.HBM)
     dma = pltpu.SemaphoreType.DMA
-    coefficients, permuted = pl.pallas_call(
+    *solved, permuted = pl.pallas_call(
         functools.partial(kernel, n),
         out_shape=(
             jax.ShapeDtypeStruct((terms, modes), f32),
+            jax.ShapeDtypeStruct((terms, modes), bf16),
             jax.ShapeDtypeStruct((count, modes), bf16),
         ),
         in_specs=[hbm] * 6,
-        out_specs=(vmem, vmem),
+        out_specs=(vmem, vmem, vmem),
         scratch_shapes=[
             pltpu.VMEM((2, chips, packet, LANES), f32),
             pltpu.VMEM((2, chips, 1, terms), f32),
@@ -488,21 +495,22 @@
             )
         ]
     )
-    steps = 4
+    width = 256
+    parts = count // width
     return pl.pallas_call(
         finish,
-        grid=(steps,),
         out_shape=(
             jax.ShapeDtypeStruct((terms, modes), f32),
             jax.ShapeDtypeStruct((terms, count), bf16),
         ),
-        in_specs=[vmem, vmem],
-        out_specs=(
-            pl.BlockSpec((terms // steps, modes), lambda step: (step, 0)),
-            pl.BlockSpec((terms, count // steps), lambda step: (0, step)),
-        ),
+        in_specs=[vmem, vmem, vmem],
+        out_specs=(hbm, hbm),
+        scratch_shapes=[
+            pltpu.VMEM((parts, terms, width), bf16),
+            dma((parts + 1,)),
+        ],
         compiler_params=pltpu.CompilerParams(vmem_limit_bytes=8 * 2**20),
-    )(coefficients, permuted)
+    )(*solved, permuted)
 
 
 def by_gathers(

time: 38.5 us -> 36.1 us (0.938)
  Pallas kernels: 37.7 us -> 35.3 us
    pallas_call x1, Pallas kernels: 34.8 us -> 33.2 us  [by_chips(): pl.pallas_call(functools.partial(kernel, n), out_shape=(jax.ShapeDtypeStr...]
    pallas_call x1, Pallas kernels: 2.91 us -> 2.08 us  [by_chips(): pl.pallas_call(finish, out_shape=(jax.ShapeDtypeStruct((terms, modes), f3...]
where the time goes in v3:
time: 36.1 us; the launch traced here: 36 us
  Pallas kernels  35.3 us (98%)
  between operations  0.64 us (2%)
    pallas_call x1, Pallas kernels, by_chips(): pl.pallas_call(functools.partial(kernel, n), out_shape=(jax.ShapeDtypeStr...  33.2 us
    pallas_call x1, Pallas kernels, by_chips(): pl.pallas_call(finish, out_shape=(jax.ShapeDtypeStruct((terms, modes), f3...  2.08 us

profile of v3, /device:TPU:9, one launch (start us, length us, event | category | flops | bytes accessed | tf_op | source)
XLA Modules:
  0.0 36.0 jit_solution(8928604153248372305)
XLA Ops:
  0.6 33.2 %shard_map.77 = (f32[256,1024]{1,0:T(8,128)S(1)}, bf16[256,1024]{1,0:T(8,128)(2,1)S(1)}, bf16[2048,1024]{1,0:T(8,128)(2,1)S(1)}) custom-call(bf16[256,1024]{1,0:T(8,128)(2,1)} %corr_hbm.1, f32[24,64]{1,0:T(8,128)} %bitcast.6, s32[16,1,256]{2,1,0:T(1,128)} %bitcast.5, s32[4,4096]{1,0:T(4,128)} %bitcast.4, s32[1,2048]{1,0:T(1,128)} %bitcast.7, ...), custom_call_target="tpu_custom_call" | custom-call | tf_op jit(solution)/shard_map/pallas_call | solution.py:440
  33.9 2.1 %shard_map.78 = (f32[256,1024]{1,0:T(8,128)}, bf16[256,2048]{1,0:T(8,128)(2,1)}) custom-call(f32[256,1024]{1,0:T(8,128)S(1)} %get-tuple-element.5.coef_in, bf16[256,1024]{1,0:T(8,128)(2,1)S(1)} %get-tuple-element.6.narrow, bf16[2048,1024]{1,0:T(8,128)(2,1)S(1)} %get-tuple-element.7.permuted), custom_call_target="tpu_custom_call" | custom-call | tf_op jit(solution)/shard_map/pallas_call | solution.py:500

commit v4 on v3

--- a/solution.py
+++ b/solution.py
@@ -88,6 +88,7 @@
     summed,
     codes,
     cells,
+    squares_ref,
     slab,
     local_sem,
     packets_send,
@@ -113,9 +114,6 @@
     low_side = chip < side
     inner = jnp.logical_and(chip >= side // 2, chip < chips - side // 2)
 
-    def peer(offset):
-        return lax.rem(me + offset, n)
-
     def chip_at(offset):
         return lax.rem(chip + offset, chips)
 
@@ -148,11 +146,12 @@
         )
 
     barrier = pltpu.get_barrier_semaphore()
-    for offset in range(1, n):
+    peers = [chip_at(offset) * 2 + core for offset in range(1, chips)]
+    for there in [*peers, chip * 2 + (1 - core)]:
         pl.semaphore_signal(
             barrier,
             inc=1,
-            device_id={"runs": peer(offset)},
+            device_id={"runs": there},
             device_id_type=pl.DeviceIdType.MESH,
         )
 
@@ -198,13 +197,13 @@
     )
     for row, lanes in norm_lanes:
         packets[core, chip, row : row + 1] = norm_rows[0:1, lanes]
-    pl.semaphore_wait(barrier, n - 1)
+    pl.semaphore_wait(barrier, chips)
 
     def packet_move(offset):
         return remote(
             packets.at[core, chip],
             packets.at[core, chip],
-            packets_send.at[offset],
+            packets_send,
             packets_recv.at[offset],
             chip_at(offset) * 2 + core,
         )
@@ -214,7 +213,7 @@
         return remote(
             corr_ref.at[:, mode_lanes(there)],
             blocks.at[term_rows(chip)],
-            blocks_send.at[offset],
+            blocks_send,
             blocks_recv.at[offset],
             there * 2 + core,
         )
@@ -231,7 +230,7 @@
         return remote(
             outgoing.at[term_rows(there)],
             summed.at[:, mode_lanes(chip)],
-            summed_send.at[offset],
+            summed_send,
             summed_recv.at[offset],
             there * 2 + core,
         )
@@ -360,9 +359,11 @@
     for step in range(1, side):
         wait_block(near_chip(step))
         fit(near_chip(step))
+    filled = jnp.where(inner, middle + 1, middle)
+    permute(middle, filled)
     for step in range(side):
-        wait_block(far_chip(side - 1 - step))
-        fit(far_chip(side - 1 - step))
+        wait_block(far_chip(step))
+        fit(far_chip(step))
 
     total_move().start()
     total_move().wait_recv()
@@ -381,7 +382,7 @@
         design[term_rows(chip), :], fitted[...]
     ).astype(jnp.bfloat16)
 
-    permute(middle, chunks)
+    permute(filled, chunks)
     own_limits = jnp.broadcast_to(STEP * penalty * weights[core, chip], (8, terms))
     limits = jnp.transpose(own_limits)[:, 0:1]
     chunk = 32
@@ -389,21 +390,39 @@
         rows = slice(start, start + chunk)
         half_corr = STEP * corr_ref[rows].astype(jnp.float32)
         coef_ref[rows] = shrink(half_corr, limits[rows]) + half_corr
-    for offset in range(1, chips):
-        summed_move(offset).wait_recv()
+    def subtract(there):
+        lanes = mode_lanes(there)
+        values = coef_ref[:, lanes] - summed[:, lanes].astype(jnp.float32) * (
+            STEP / runs
+        )
+        coef_ref[:, lanes] = values
+        squares = values * values
+        parts = [squares[:, at : at + LANES] for at in range(0, width, LANES)]
+        return functools.reduce(jnp.add, parts)
+
+    squares_ref[...] = subtract(chip)
+    arrivals = [near_chip(step) for step in range(1, side)]
+    arrivals += [far_chip(step) for step in range(side)]
+    for there in arrivals:
+        summed_move(lax.rem(chip - there + chips, chips)).wait_recv()
+        squares_ref[...] += subtract(there)
+    length = jnp.sqrt(jnp.sum(squares_ref[...], axis=1, keepdims=True) + EPSILON)
+    factor = jnp.maximum(0.0, 1.0 - limits / length)
     for start in range(0, terms, chunk):
         rows = slice(start, start + chunk)
-        step_sum = summed[rows].astype(jnp.float32) * (STEP / runs)
-        coefficients = shrink(coef_ref[rows] - step_sum, limits[rows])
+        coefficients = coef_ref[rows] * factor[rows]
         coef_ref[rows] = coefficients
         narrow_ref[rows] = coefficients.astype(jnp.bfloat16)
 
     packets_relay.wait_send()
-    for offset in range(1, chips):
-        packet_move(offset).wait_send()
-        block_move(offset).wait_send()
-        summed_move(offset).wait_send()
     total_move().wait_send()
+    others = chips - 1
+    partner = chip * 2 + (1 - core)
+    sent = packets.at[core, 0:others]
+    remote(sent, sent, packets_send, relay_recv, partner).wait_send()
+    sent = outgoing.at[0 : others * terms]
+    remote(sent, sent, blocks_send, relay_recv, partner).wait_send()
+    remote(sent, sent, summed_send, relay_recv, partner).wait_send()
 
 
 def finish(coef_in, narrow, permuted, coef_hbm, lift_hbm, lift, sems):
@@ -466,17 +485,18 @@
             pltpu.VMEM((terms, modes), bf16),
             pltpu.VMEM((lane_terms, 8), jnp.int32),
             pltpu.VMEM((count, 8), jnp.int32),
+            pltpu.VMEM((terms, LANES), f32),
             pltpu.VMEM(slab_modes.shape, bf16),
             dma((7,)),
-            dma((chips,)),
+            dma,
             dma((chips,)),
             dma,
             dma,
-            dma((chips,)),
+            dma,
             dma((chips,)),
             dma,
             dma,
-            dma((chips,)),
+            dma,
             dma((chips,)),
         ],
         compiler_params=pltpu.CompilerParams(
@@ -495,7 +515,7 @@
             )
         ]
     )
-    width = 256
+    width = 512
     parts = count // width
     return pl.pallas_call(
         finish,

time: 36.1 us -> 36 us (level)
  no operation moved by 1% of the time
where the time goes in v4:
time: 36 us; the launch traced here: 35.9 us
  Pallas kernels  35.2 us (98%)
  between operations  0.64 us (2%)
    pallas_call x1, Pallas kernels, by_chips(): pl.pallas_call(functools.partial(kernel, n), out_shape=(jax.ShapeDtypeStr...  33.2 us
    pallas_call x1, Pallas kernels, by_chips(): pl.pallas_call(finish, out_shape=(jax.ShapeDtypeStruct((terms, modes), f3...  2.03 us

profile of v4, /device:TPU:9, one launch (start us, length us, event | category | flops | bytes accessed | tf_op | source)
XLA Modules:
  0.0 35.9 jit_solution(6029454746914978929)
XLA Ops:
  0.6 33.2 %shard_map.77 = (f32[256,1024]{1,0:T(8,128)S(1)}, bf16[256,1024]{1,0:T(8,128)(2,1)S(1)}, bf16[2048,1024]{1,0:T(8,128)(2,1)S(1)}) custom-call(bf16[256,1024]{1,0:T(8,128)(2,1)} %corr_hbm.1, f32[24,64]{1,0:T(8,128)} %bitcast.6, s32[16,1,256]{2,1,0:T(1,128)} %bitcast.5, s32[4,4096]{1,0:T(4,128)} %bitcast.4, s32[1,2048]{1,0:T(1,128)} %bitcast.7, ...), custom_call_target="tpu_custom_call" | custom-call | tf_op jit(solution)/shard_map/pallas_call | solution.py:459
  33.8 2.0 %shard_map.78 = (f32[256,1024]{1,0:T(8,128)}, bf16[256,2048]{1,0:T(8,128)(2,1)}) custom-call(f32[256,1024]{1,0:T(8,128)S(1)} %get-tuple-element.5.coef_in, bf16[256,1024]{1,0:T(8,128)(2,1)S(1)} %get-tuple-element.6.narrow, bf16[2048,1024]{1,0:T(8,128)(2,1)S(1)} %get-tuple-element.7.permuted), custom_call_target="tpu_custom_call" | custom-call | tf_op jit(solution)/shard_map/pallas_call | solution.py:520
